TPU v7x, 32 devices: a whole 2x2x4 slice. The times are simulated.
32 devices in a mesh: seq: 8 (over z, y), fsdp: 4 (over x, core).
Axes of the slice: x: 2, y: 2, z: 4, core: 2. Of those that a mesh axis runs over, the one named last changes fastest.
Arguments:
- hidden_in: bfloat16 [4, 1024, 2048], P('fsdp', 'seq'), may hold values from -18 to 18
- ln1_gain: bfloat16 [2048], P(('seq', 'fsdp')), may hold values from 0.5 to 1.5
- ln1_bias: bfloat16 [2048], P(('seq', 'fsdp')), may hold values from -1.1953125 to 1.1953125
- qkv_weight: bfloat16 [2048, 6144], P(('seq', 'fsdp')), may hold values from -0.125 to 0.125
- qkv_bias: bfloat16 [3, 2048], P(None, ('seq', 'fsdp')), may hold values from -3 to 3
- out_weight: bfloat16 [2048, 2048], P(('seq', 'fsdp')), may hold values from -3 to 3
- ln2_gain: bfloat16 [2048], P(('seq', 'fsdp')), may hold values from 0.5 to 1.5
- ln2_bias: bfloat16 [2048], P(('seq', 'fsdp')), may hold values from -1.1953125 to 1.1953125
- gate_weight: bfloat16 [2048, 5632], P(('seq', 'fsdp')), may hold values from -0.125 to 0.125
- up_weight: bfloat16 [2048, 5632], P(('seq', 'fsdp')), may hold values from -0.125 to 0.125
- down_weight: bfloat16 [5632, 2048], P(('seq', 'fsdp')), may hold values from -0.078125 to 0.078125
- seq_lengths: int32 [4, 3], P('fsdp'), may hold values from 1 to 512, 640 in all within a row
- deal_order: int32 [4, 1024], P('fsdp'), may hold values from 0 to 1023, each once within a row
- out_grad: bfloat16 [4, 1024, 2048], P('fsdp', 'seq'), may hold values from -6 to 6
Outputs:
- layer_out: bfloat16 [4, 1024, 2048], P('fsdp', 'seq')
- input_grad: float32 [4, 1024, 2048], P('fsdp', 'seq')
- ln1_gain_grad: float32 [2048], P(('seq', 'fsdp'))
- ln1_bias_grad: float32 [2048], P(('seq', 'fsdp'))
- qkv_weight_grad: float32 [2048, 6144], P(('seq', 'fsdp'))
- qkv_bias_grad: float32 [3, 2048], P(None, ('seq', 'fsdp'))
- out_weight_grad: float32 [2048, 2048], P(('seq', 'fsdp'))
- ln2_gain_grad: float32 [2048], P(('seq', 'fsdp'))
- ln2_bias_grad: float32 [2048], P(('seq', 'fsdp'))
- gate_weight_grad: float32 [2048, 5632], P(('seq', 'fsdp'))
- up_weight_grad: float32 [2048, 5632], P(('seq', 'fsdp'))
- down_weight_grad: float32 [5632, 2048], P(('seq', 'fsdp'))
- branch_rms: float32 [3], replicated
Inputs may be any that keep to these rules, and one draw needn't show every extreme that they name: `seq_lengths`: each group's lengths sum to 640, and its longest is exactly 512. `deal_order`: each group's row is a permutation of its positions.
All inputs are finite; a program needn't handle non-finite values.
Results may differ from a plain program's by a relative error of at most 0.00705.
The roundings to bfloat16 on the way count: a program that leaves them out, or rounds other values in their place, can miss the bound.
Values may be sent and summed in bfloat16 or wider, within the bound.
A program may use at most 384 MiB of HBM per device.

v0:
```python
import jax
import jax.numpy as jnp
from jax import lax
from jax.sharding import PartitionSpec as P

HEAD_DIM = 64
ROT = 16
EPS = 1e-05


def normalize(values):
    center = values - jnp.mean(values, -1, keepdims=True)
    spread = jnp.mean(center * center, -1, keepdims=True)
    rstd = lax.rsqrt(spread + EPS)
    return (center * rstd, rstd)


def norm_back(grad, normed, rstd, gain):
    scaled = grad * gain
    inner = (
        scaled
        - jnp.mean(scaled, -1, keepdims=True)
        - normed * jnp.mean(scaled * normed, -1, keepdims=True)
    )
    return (rstd * inner, jnp.sum(grad * normed, 0), jnp.sum(grad, 0))


def segment_of(pos, lengths):
    nseg = lengths.shape[0]
    ends = jnp.cumsum(lengths)
    seg = jnp.sum((pos[:, None] >= ends[None, :]).astype(jnp.int32), 1)
    starts = jnp.concatenate([jnp.zeros((1,), jnp.int32), ends[:-1]])
    start = jnp.sum(
        jnp.where(seg[:, None] == jnp.arange(nseg, dtype=jnp.int32)[None, :], starts[None, :], 0), 1
    )
    start = jnp.where(seg < nseg, start, pos)
    return (seg, start)


def rotate(values, rel, sign):
    count = values.shape[0]
    view = values.reshape(count, -1, HEAD_DIM)
    half = ROT // 2
    freq = 10000.0 ** (-2.0 * jnp.arange(half, dtype=jnp.float32) / ROT)
    angle = rel[:, None] * freq[None, :]
    cosine = jnp.cos(angle)[:, None, :]
    sine = jnp.sin(angle)[:, None, :]
    first = view[..., :half]
    second = view[..., half:ROT]
    turned = jnp.concatenate(
        [
            first * cosine - sign * second * sine,
            second * cosine + sign * first * sine,
            view[..., ROT:],
        ],
        -1,
    )
    return turned.reshape(count, -1)


def outer(left, right):
    return lax.dot_general(
        left, right, (((0,), (0,)), ((), ())), preferred_element_type=jnp.float32
    )


def times_transposed(left, right):
    return lax.dot_general(
        left, right, (((1,), (1,)), ((), ())), preferred_element_type=jnp.float32
    )


def mlp_forward(gate, upper):
    sigma = jax.nn.sigmoid(gate)
    return ((gate * sigma * upper).astype(jnp.bfloat16), sigma)


def mlp_backward(hidden_grad, gate, upper, sigma):
    up_act = (hidden_grad * gate * sigma).astype(jnp.bfloat16)
    gate_act = (hidden_grad * upper * sigma * (1.0 + gate * (1.0 - sigma))).astype(jnp.bfloat16)
    return (gate_act, up_act)


def body(
    hidden_in,
    ln1_gain,
    ln1_bias,
    qkv_weight,
    qkv_bias,
    out_weight,
    ln2_gain,
    ln2_bias,
    gate_weight,
    up_weight,
    down_weight,
    seq_lengths,
    deal_order,
    out_grad,
):
    rows = hidden_in.shape[1]
    width = hidden_in.shape[2]
    stream = hidden_in[0].astype(jnp.float32)
    cotangent = out_grad[0].astype(jnp.float32)
    order = deal_order[0]
    lengths = seq_lengths[0]
    nseg = lengths.shape[0]
    group_rows = order.shape[0]
    valid_rows = group_rows * 5 // 8
    longest = valid_rows * 4 // 5
    blk = min(512, group_rows)
    keys = min(group_rows, longest + blk)
    nblocks = group_rows // blk
    scale = HEAD_DIM ** (-0.5)
    local_pos = lax.dynamic_slice_in_dim(order, lax.axis_index("seq") * rows, rows)
    local_seg, local_start = segment_of(local_pos, lengths)
    rel = (local_pos - local_start).astype(jnp.float32)
    valid = (local_pos < valid_rows).astype(jnp.float32)[:, None]
    normed1, rstd1 = normalize(stream)
    inverse = (
        jnp.zeros((group_rows,), jnp.int32).at[order].set(jnp.arange(group_rows, dtype=jnp.int32))
    )
    seg_p, start_p = segment_of(jnp.arange(group_rows, dtype=jnp.int32), lengths)

    def to_pack(values):
        heads_here = values.shape[1] // HEAD_DIM
        return values[inverse].reshape(group_rows, heads_here, HEAD_DIM)

    def window(index, packed):
        query_p, key_p, value_p = packed
        first = index * blk
        key_first = jnp.clip(jnp.minimum(start_p[first], group_rows - keys), 0, group_rows - keys)
        qpos = first + jnp.arange(blk, dtype=jnp.int32)
        kpos = key_first + jnp.arange(keys, dtype=jnp.int32)
        qseg = lax.dynamic_slice_in_dim(seg_p, first, blk)
        kseg = lax.dynamic_slice_in_dim(seg_p, key_first, keys)
        allowed = (qseg[:, None] == kseg[None, :]) & (qseg[:, None] < nseg) & (
            kpos[None, :] <= qpos[:, None]
        ) | (kpos[None, :] == qpos[:, None])
        qblock = lax.dynamic_slice_in_dim(query_p, first, blk)
        kblock = lax.dynamic_slice_in_dim(key_p, key_first, keys)
        vblock = lax.dynamic_slice_in_dim(value_p, key_first, keys)
        scores = (
            jnp.einsum("qhd,khd->hqk", qblock, kblock, preferred_element_type=jnp.float32) * scale
        )
        scores = jnp.where(allowed[None], scores, -1e30)
        return (first, key_first, qblock, kblock, vblock, scores)

    def fetch_full(gain, shift, first_w, middle_w, last_w):
        return (
            lax.all_gather(gain, ("seq", "fsdp"), axis=0, tiled=True),
            lax.all_gather(shift, ("seq", "fsdp"), axis=0, tiled=True),
            lax.all_gather(first_w, ("seq", "fsdp"), axis=0, tiled=True),
            lax.all_gather(middle_w, ("seq", "fsdp"), axis=0, tiled=True),
            lax.all_gather(last_w, ("seq", "fsdp"), axis=0, tiled=True),
        )

    def reduce_full(gain, shift, first_w, middle_w, last_w):
        return (
            lax.psum_scatter(gain, ("seq", "fsdp"), scatter_dimension=0, tiled=True),
            lax.psum_scatter(shift, ("seq", "fsdp"), scatter_dimension=0, tiled=True),
            lax.psum_scatter(first_w, ("seq", "fsdp"), scatter_dimension=0, tiled=True),
            lax.psum_scatter(middle_w, ("seq", "fsdp"), scatter_dimension=0, tiled=True),
            lax.psum_scatter(last_w, ("seq", "fsdp"), scatter_dimension=0, tiled=True),
        )

    gain1, shift1, qkv_w, qkv_b, out_w = fetch_full(
        ln1_gain, ln1_bias, qkv_weight, qkv_bias.T, out_weight
    )
    qkv_shift = qkv_b.T.reshape(-1).astype(jnp.float32)
    first_in = (normed1 * gain1.astype(jnp.float32) + shift1.astype(jnp.float32)).astype(
        jnp.bfloat16
    )
    qkv = jnp.dot(first_in, qkv_w, preferred_element_type=jnp.float32) + qkv_shift
    query = rotate(qkv[:, :width], rel, 1.0).astype(jnp.bfloat16)
    keyset = rotate(qkv[:, width : 2 * width], rel, 1.0).astype(jnp.bfloat16)
    valueset = qkv[:, 2 * width :].astype(jnp.bfloat16)
    query, keyset, valueset = (query, keyset, valueset)
    query_h = lax.all_to_all(query, "seq", split_axis=1, concat_axis=0, tiled=True)
    key_h = lax.all_to_all(keyset, "seq", split_axis=1, concat_axis=0, tiled=True)
    value_h = lax.all_to_all(valueset, "seq", split_axis=1, concat_axis=0, tiled=True)
    packed = (to_pack(query_h), to_pack(key_h), to_pack(value_h))

    def attend_block(index):
        first, key_first, qblock, kblock, vblock, scores = window(index, packed)
        top = jnp.max(scores, -1, keepdims=True)
        expo = jnp.exp(scores - top)
        total = jnp.sum(expo, -1, keepdims=True)
        probs = (expo / total).astype(jnp.bfloat16)
        mixed = jnp.einsum("hqk,khd->qhd", probs, vblock, preferred_element_type=jnp.float32)
        return (mixed, (top + jnp.log(total))[..., 0])

    mixed_all, lse_all = lax.map(attend_block, jnp.arange(nblocks, dtype=jnp.int32))
    mixed_pack = mixed_all.reshape(group_rows, -1)
    heads_out = lax.all_to_all(
        mixed_pack[order].astype(jnp.bfloat16), "seq", split_axis=0, concat_axis=1, tiled=True
    )
    heads_out, packed, lse_all = (heads_out, packed, lse_all)
    attn = jnp.dot(heads_out, out_w, preferred_element_type=jnp.float32)
    resid = stream + attn
    gain2, shift2, gate_w, up_w, down_w = fetch_full(
        ln2_gain, ln2_bias, gate_weight, up_weight, down_weight
    )
    normed2, rstd2 = normalize(resid)
    second_in = (normed2 * gain2.astype(jnp.float32) + shift2.astype(jnp.float32)).astype(
        jnp.bfloat16
    )
    gate = jnp.dot(second_in, gate_w, preferred_element_type=jnp.float32)
    upper = jnp.dot(second_in, up_w, preferred_element_type=jnp.float32)
    hidden, sigma = mlp_forward(gate, upper)
    mlp = jnp.dot(hidden, down_w, preferred_element_type=jnp.float32)
    result = resid + mlp
    sums = lax.psum(
        (
            jnp.sum(valid * result * result),
            jnp.sum(valid * attn * attn),
            jnp.sum(valid * mlp * mlp),
        ),
        ("seq", "fsdp"),
    )
    count = valid_rows * lax.axis_size("fsdp") * width
    rms = jnp.sqrt(jnp.stack(sums) / count)
    gain2, shift2, gate_w, up_w, down_w = fetch_full(
        ln2_gain, ln2_bias, gate_weight, up_weight, down_weight
    )
    mlp_grad = cotangent.astype(jnp.bfloat16)
    down_grad = outer(hidden, mlp_grad)
    hidden_grad = times_transposed(mlp_grad, down_w)
    gate_act, up_act = mlp_backward(hidden_grad, gate, upper, sigma)
    gate_grad = outer(second_in, gate_act)
    up_grad = outer(second_in, up_act)
    second_grad = times_transposed(gate_act, gate_w) + times_transposed(up_act, up_w)
    resid_part, gain2_grad, shift2_grad = norm_back(
        second_grad, normed2, rstd2, gain2.astype(jnp.float32)
    )
    resid_grad = cotangent + resid_part
    mlp_shards = reduce_full(gain2_grad, shift2_grad, gate_grad, up_grad, down_grad)
    gain1, shift1, qkv_w, qkv_b, out_w = fetch_full(
        ln1_gain, ln1_bias, qkv_weight, qkv_bias.T, out_weight
    )
    attn_grad = resid_grad.astype(jnp.bfloat16)
    out_grad_w = outer(heads_out, attn_grad)
    mixed_grad = times_transposed(attn_grad, out_w).astype(jnp.bfloat16)
    mixed_grad_p = to_pack(
        lax.all_to_all(mixed_grad, "seq", split_axis=1, concat_axis=0, tiled=True)
    )

    def back_block(index, carry):
        query_acc, key_acc, value_acc = carry
        first, key_first, qblock, kblock, vblock, scores = window(index, packed)
        probs = jnp.exp(scores - lse_all[index][:, :, None])
        dblock = lax.dynamic_slice_in_dim(mixed_grad_p, first, blk)
        value_part = jnp.einsum(
            "hqk,qhd->khd", probs.astype(jnp.bfloat16), dblock, preferred_element_type=jnp.float32
        )
        prob_grad = jnp.einsum("qhd,khd->hqk", dblock, vblock, preferred_element_type=jnp.float32)
        inner = jnp.sum(probs * prob_grad, -1, keepdims=True)
        score_grad = (probs * (prob_grad - inner)).astype(jnp.bfloat16)
        query_part = (
            jnp.einsum("hqk,khd->qhd", score_grad, kblock, preferred_element_type=jnp.float32)
            * scale
        )
        key_part = (
            jnp.einsum("hqk,qhd->khd", score_grad, qblock, preferred_element_type=jnp.float32)
            * scale
        )
        query_acc = lax.dynamic_update_slice_in_dim(query_acc, query_part, first, 0)
        key_old = lax.dynamic_slice_in_dim(key_acc, key_first, keys)
        key_acc = lax.dynamic_update_slice_in_dim(key_acc, key_old + key_part, key_first, 0)
        value_old = lax.dynamic_slice_in_dim(value_acc, key_first, keys)
        value_acc = lax.dynamic_update_slice_in_dim(value_acc, value_old + value_part, key_first, 0)
        return (query_acc, key_acc, value_acc)

    zeros = jnp.zeros(packed[0].shape, jnp.float32)
    query_acc, key_acc, value_acc = lax.fori_loop(0, nblocks, back_block, (zeros, zeros, zeros))

    def to_dealt(values):
        return values.reshape(group_rows, -1)[order].astype(jnp.bfloat16)

    query_g = lax.all_to_all(to_dealt(query_acc), "seq", split_axis=0, concat_axis=1, tiled=True)
    key_g = lax.all_to_all(to_dealt(key_acc), "seq", split_axis=0, concat_axis=1, tiled=True)
    value_g = lax.all_to_all(to_dealt(value_acc), "seq", split_axis=0, concat_axis=1, tiled=True)
    qkv_act = jnp.concatenate(
        [
            rotate(query_g.astype(jnp.float32), rel, -1.0),
            rotate(key_g.astype(jnp.float32), rel, -1.0),
            value_g.astype(jnp.float32),
        ],
        1,
    ).astype(jnp.bfloat16)
    qkv_bias_grad = jnp.sum(qkv_act.astype(jnp.float32), 0).reshape(3, width).T
    qkv_grad = outer(first_in, qkv_act)
    first_grad = times_transposed(qkv_act, qkv_w)
    input_part, gain1_grad, shift1_grad = norm_back(
        first_grad, normed1, rstd1, gain1.astype(jnp.float32)
    )
    input_grad = resid_grad + input_part
    attn_shards = reduce_full(gain1_grad, shift1_grad, qkv_grad, qkv_bias_grad, out_grad_w)
    return (
        result.astype(jnp.bfloat16)[None],
        input_grad[None],
        attn_shards[0],
        attn_shards[1],
        attn_shards[2],
        attn_shards[3].T,
        attn_shards[4],
        mlp_shards[0],
        mlp_shards[1],
        mlp_shards[2],
        mlp_shards[3],
        mlp_shards[4],
        rms,
    )


def solution(mesh):
    in_specs = (
        P("fsdp", "seq", None),
        P(("seq", "fsdp")),
        P(("seq", "fsdp")),
        P(("seq", "fsdp"), None),
        P(None, ("seq", "fsdp")),
        P(("seq", "fsdp"), None),
        P(("seq", "fsdp")),
        P(("seq", "fsdp")),
        P(("seq", "fsdp"), None),
        P(("seq", "fsdp"), None),
        P(("seq", "fsdp"), None),
        P("fsdp", None),
        P("fsdp", None),
        P("fsdp", "seq", None),
    )
    out_specs = (
        P("fsdp", "seq", None),
        P("fsdp", "seq", None),
        P(("seq", "fsdp")),
        P(("seq", "fsdp")),
        P(("seq", "fsdp"), None),
        P(None, ("seq", "fsdp")),
        P(("seq", "fsdp"), None),
        P(("seq", "fsdp")),
        P(("seq", "fsdp")),
        P(("seq", "fsdp"), None),
        P(("seq", "fsdp"), None),
        P(("seq", "fsdp"), None),
        P(),
    )
    return jax.shard_map(body, mesh=mesh, in_specs=in_specs, out_specs=out_specs, check_vma=False)
```

profile of v0, /device:TPU:1, one launch (start us, length us, event | category | flops | bytes accessed | tf_op | source)
XLA Modules:
  0.0 3154.0 jit_solution(16658378083250577882)
XLA Ops:
  11.4 43.8 %all-gather = bf16[32,64,3]{1,2,0:T(4,128)(2,1)S(1)} all-gather(bf16[1,64,3]{1,2,0:T(4,128)(2,1)} %bitcast.252), channel_id=1, replica_groups=mesh['seq'=8,'fsdp'=4] {'seq','fsdp'}, dimensions={0}, use_global_device_ids=true | all-gather | bytes 12672 | tf_op jit(solution)/shard_map/all_gather | solution.py:153
  58.7 37.6 %all-reduce.9 = (bf16[2048]{0:T(1024)(128)(2,1)S(1)}, bf16[2048]{0:T(1024)(128)(2,1)S(1)}, bf16[2048]{0:T(1024)(128)(2,1)S(1)}, bf16[2048]{0:T(1024)(128)(2,1)S(1)}) all-reduce(bf16[2048]{0:T(1024)(128)(2,1)S(1)} %dynamic-update-slice.1, bf16[2048]{0:T(1024)(128)(2,1)S(1)} %dynamic-update-slice, ...), channel_id=1, replica_groups=mesh['seq'=8,'fsdp'=4] {'seq','fsdp'}, use_global_device_ids=true, to_apply=%add.1 | all-reduce | flops 8192 | bytes 32768
  100.1 69.8 %all-gather.7.cloned.1.call-done = bf16[2048,6144]{1,0:T(8,128)(2,1)} async-done(((bf16[64,6144]{1,0:T(8,128)(2,1)}), bf16[2048,6144]{1,0:T(8,128)(2,1)}) %all-gather.7.cloned.1.call-update) | async-done | bytes 25165840 | tf_op jit(solution)/shard_map/all_gather | solution.py:152
  169.9 10.1 convolution_add_fusion
  187.0 20.9 all_to_all.116
  216.9 11.1 all-to-all-done.1
  227.9 13.6 all-to-all-start.2
  266.7 22.6 while.30
  302.5 27.9 all-to-all-done.3
  337.5 81.7 %all-gather.11.cloned.1.call-done = bf16[2048,5632]{1,0:T(8,128)(2,1)} async-done(((bf16[64,5632]{1,0:T(8,128)(2,1)}), bf16[2048,5632]{1,0:T(8,128)(2,1)}) %all-gather.11.cloned.1.call-update) | async-done | bytes 23068688 | tf_op jit(solution)/shard_map/all_gather | solution.py:152
  419.2 12.5 fusion.76
  431.7 133.0 %all-gather.13.cloned.1.call-done = bf16[2048,5632]{1,0:T(8,128)(2,1)} async-done(((bf16[64,5632]{1,0:T(8,128)(2,1)}), bf16[2048,5632]{1,0:T(8,128)(2,1)}) %all-gather.13.cloned.1.call-update) | async-done | bytes 23068688 | tf_op jit(solution)/shard_map/all_gather | solution.py:153
  564.7 12.3 fusion.77
  577.0 133.2 %all-gather.15.cloned.1.call-done = bf16[5632,2048]{1,0:T(8,128)(2,1)} async-done(((bf16[176,2048]{1,0:T(8,128)(2,1)}), bf16[5632,2048]{1,0:T(8,128)(2,1)}) %all-gather.15.cloned.1.call-update) | async-done | bytes 23068688 | tf_op jit(solution)/shard_map/all_gather | solution.py:154
  710.2 15.6 multiply_convert_fusion.1
  725.8 13.4 fusion.78
  739.2 12.2 convolution_add_fusion.1
  751.5 13.5 fusion.53
  773.1 13.7 all-to-all-done.4
  794.7 44.1 %while.31 = (s32[]{:T(128)}, bf16[1024,4,64]{0,2,1:T(8,128)(2,1)}, f32[1024,4,64]{0,2,1:T(8,128)S(1)}, f32[1024,4,64]{0,2,1:T(8,128)}, s32[1024]{0:T(1024)S(1)},...) while((s32[]{:T(128)}, bf16[1024,4,64]{0,2,1:T(8,128)(2,1)}, ...), condition=%wide.region_18.19_spmd.clone, body=%wide.region_16.18_spmd.clone.sunk | while | flops 1378222080 | bytes 164707824 | solution.py:274
  886.1 12.8 all-to-all-done.7
  910.1 20.8 fusion.69
  932.5 18.0 fusion.79
  951.9 18.0 fusion.80
  971.3 18.0 fusion.56
  990.7 20.7 fusion.51
  1011.4 44.7 %all-reduce.8 = (f32[2048]{0:T(1024)S(1)}, f32[2048]{0:T(1024)S(1)}, f32[2048]{0:T(1024)S(1)}, f32[2048]{0:T(1024)S(1)}, f32[1]{0:T(128)}, /*index=5*/f32[1]{0:T(128)}, f32[1]{0:T(128)}) all-reduce(f32[2048]{0:T(1024)S(1)} %get-tuple-element.310, ...), channel_id=2, replica_groups=mesh['seq'=8,'fsdp'=4] {'seq','fsdp'}, use_global_device_ids=true, to_apply=%region_22.23.clone | all-reduce | flops 8195 | bytes 65560
  1065.1 153.7 %reduce-scatter.11.cloned.1.call-done = f32[64,2048]{1,0:T(8,128)} async-done(((f32[2048,2048]{1,0:T(8,128)}), f32[64,2048]{1,0:T(8,128)}) %reduce-scatter.11.cloned.1.call-update) | async-done | bytes 524304 | tf_op jit(solution)/shard_map/reduce_scatter | solution.py:163
  1218.8 441.8 %reduce-scatter.9.cloned.1.call-done = f32[64,6144]{1,0:T(8,128)} async-done(((f32[2048,6144]{1,0:T(8,128)}), f32[64,6144]{1,0:T(8,128)}) %reduce-scatter.9.cloned.1.call-update) | async-done | bytes 1572880 | tf_op jit(solution)/shard_map/reduce_scatter | solution.py:161
  1660.6 494.7 %reduce-scatter.13.cloned.1.call-done = f32[64,5632]{1,0:T(8,128)} async-done(((f32[2048,5632]{1,0:T(8,128)}), f32[64,5632]{1,0:T(8,128)}) %reduce-scatter.13.cloned.1.call-update) | async-done | bytes 1441808 | tf_op jit(solution)/shard_map/reduce_scatter | solution.py:161
  2155.3 495.9 %reduce-scatter.15.cloned.1.call-done = f32[64,5632]{1,0:T(8,128)} async-done(((f32[2048,5632]{1,0:T(8,128)}), f32[64,5632]{1,0:T(8,128)}) %reduce-scatter.15.cloned.1.call-update) | async-done | bytes 1441808 | tf_op jit(solution)/shard_map/reduce_scatter | solution.py:162
  2651.2 496.0 %reduce-scatter.17.cloned.1.call-done = f32[176,2048]{1,0:T(8,128)} async-done(((f32[5632,2048]{1,0:T(8,128)}), f32[176,2048]{1,0:T(8,128)}) %reduce-scatter.17.cloned.1.call-update) | async-done | bytes 1441808 | tf_op jit(solution)/shard_map/reduce_scatter | solution.py:163
  (306 shorter events, 223.9 us)
Async XLA Ops:
  7.2 91.9 %copy-start.3 = (bf16[1,128,2048]{2,1,0:T(8,128)(2,1)S(1)}, bf16[1,128,2048]{2,1,0:T(8,128)(2,1)}, u32[]{:S(2)}) copy-start(bf16[1,128,2048]{2,1,0:T(8,128)(2,1)} %param.18) | copy-start | bytes 1572868
  7.2 162.7 %all-gather.7.cloned.1.call-start = ((), (), s32[]{:S(2)}) async-start(), calls=%async_computation.14 | async-start | bytes 25952256 | tf_op jit(solution)/shard_map/all_gather | solution.py:152
  7.9 294.5 %all-gather.9.cloned.1.call-start = ((), (), s32[]{:S(2)}) async-start(), calls=%async_computation.15 | async-start | bytes 8650752 | tf_op jit(solution)/shard_map/all_gather | solution.py:154
  8.7 410.5 %all-gather.11.cloned.1.call-start = ((), (), s32[]{:S(2)}) async-start(), calls=%async_computation.16 | async-start | bytes 23789568 | tf_op jit(solution)/shard_map/all_gather | solution.py:152
  9.4 555.3 %all-gather.13.cloned.1.call-start = ((), (), s32[]{:S(2)}) async-start(), calls=%async_computation.17 | async-start | bytes 23789568 | tf_op jit(solution)/shard_map/all_gather | solution.py:153
  10.0 700.2 %all-gather.15.cloned.1.call-start = ((), (), s32[]{:S(2)}) async-start(), calls=%async_computation.18 | async-start | bytes 23789568 | tf_op jit(solution)/shard_map/all_gather | solution.py:154
  96.4 83.7 %copy-start.33 = (f32[2048]{0:T(1024)}, f32[2048]{0:T(1024)S(1)}, u32[]{:S(2)}) copy-start(f32[2048]{0:T(1024)S(1)} %convert_element_type.172) | copy-start | bytes 24580
  96.4 83.7 %copy-start.29 = (f32[2048]{0:T(1024)}, f32[2048]{0:T(1024)S(1)}, u32[]{:S(2)}) copy-start(f32[2048]{0:T(1024)S(1)} %convert_element_type.171) | copy-start | bytes 24580
  99.1 81.0 %copy-start.41 = (f32[128]{0:T(128)}, f32[128]{0:T(128)S(1)}, u32[]{:S(2)}) copy-start(f32[128]{0:T(128)S(1)} %broadcast_multiply_fusion.6) | copy-start | bytes 1540
  99.4 80.7 %copy-start.45 = (f32[128]{0:T(128)}, f32[128]{0:T(128)S(1)}, u32[]{:S(2)}) copy-start(f32[128]{0:T(128)S(1)} %add_rsqrt_fusion.1) | copy-start | bytes 1540
  100.1 84.9 %copy-start.39 = (f32[128,8]{0,1:T(8,128)}, f32[128,8]{0,1:T(8,128)S(1)}, u32[]{:S(2)}) copy-start(f32[128,8]{0,1:T(8,128)S(1)} %get-tuple-element.405) | copy-start | bytes 12292
  185.0 56.6 %copy-start.48 = (s32[1,1024]{1,0:T(1,128)S(1)}, s32[1,1024]{1,0:T(1,128)}, u32[]{:S(2)}) copy-start(s32[1,1024]{1,0:T(1,128)} %param.30) | copy-start | bytes 12292
  207.8 20.1 all-to-all-start.1
  227.9 34.5 %all-to-all-start.2 = ((bf16[128,8,256]{2,0,1:T(8,128)(2,1)}), bf16[128,8,256]{2,0,1:T(8,128)(2,1)S(1)}, u32[]{:S(2)}, u32[]{:S(2)}) async-start(bf16[128,8,256]{2,0,1:T(8,128)(2,1)} %bitcast.173), calls=%async_computation.2 | async-start | bytes 1048576 | tf_op jit(solution)/shard_map/all_to_all | solution.py:180
  247.0 46.7 %copy-start.35 = (s32[1024]{0:T(1024)}, s32[1024]{0:T(1024)S(1)}, u32[]{:S(2)}) copy-start(s32[1024]{0:T(1024)S(1)} %broadcast_clamp_fusion) | copy-start | bytes 12292
  298.6 31.7 %all-to-all-start.3 = ((bf16[8,128,256]{1,2,0:T(8,128)(2,1)}), bf16[8,128,256]{1,2,0:T(8,128)(2,1)S(1)}, u32[]{:S(2)}, u32[]{:S(2)}) async-start(bf16[8,128,256]{1,2,0:T(8,128)(2,1)} %copy.115), calls=%async_computation.3 | async-start | bytes 1048576 | tf_op jit(solution)/shard_map/all_to_all | solution.py:194
  337.5 227.2 %copy-start.7 = (bf16[128,2048]{1,0:T(8,128)(2,1)}, bf16[128,2048]{1,0:T(8,128)(2,1)S(1)}, u32[]{:S(2)}) copy-start(bf16[128,2048]{1,0:T(8,128)(2,1)S(1)} %add_convert_fusion) | copy-start | bytes 1572868
  765.6 21.1 copy-start.38
  769.4 17.4 all-to-all-start.4
  794.7 44.3 %copy-start.36 = (s32[1024]{0:T(1024)S(1)}, s32[1024]{0:T(1024)}, u32[]{:S(2)}) copy-start(s32[1024]{0:T(1024)} %copy-done.35) | copy-start | bytes 12292
  843.9 18.0 all-to-all-start.6
  862.0 18.7 all-to-all-start.5
  880.6 18.3 all-to-all-start.7
  885.5 178.2 %reduce-scatter.19.cloned.1.call-start = ((), (), s32[]{:S(2)}) async-start(), calls=%async_computation.24 | async-start | bytes 1081344
  886.0 23.1 copy-start.20
  886.1 23.1 copy-start.22
  900.9 317.9 %reduce-scatter.11.cloned.1.call-start = ((), (), s32[]{:S(2)}) async-start(), calls=%async_computation.20 | async-start | bytes 17301504 | tf_op jit(solution)/shard_map/reduce_scatter | solution.py:163
  909.1 751.5 %reduce-scatter.9.cloned.1.call-start = ((), (), s32[]{:S(2)}) async-start(), calls=%async_computation.19 | async-start | bytes 51904512 | tf_op jit(solution)/shard_map/reduce_scatter | solution.py:161
  931.0 1224.3 %reduce-scatter.13.cloned.1.call-start = ((), (), s32[]{:S(2)}) async-start(), calls=%async_computation.21 | async-start | bytes 47579136 | tf_op jit(solution)/shard_map/reduce_scatter | solution.py:161
  950.5 1700.7 %reduce-scatter.15.cloned.1.call-start = ((), (), s32[]{:S(2)}) async-start(), calls=%async_computation.22 | async-start | bytes 47579136 | tf_op jit(solution)/shard_map/reduce_scatter | solution.py:162
  969.9 2177.4 %reduce-scatter.17.cloned.1.call-start = ((), (), s32[]{:S(2)}) async-start(), calls=%async_computation.23 | async-start | bytes 47579136 | tf_op jit(solution)/shard_map/reduce_scatter | solution.py:163
  990.7 20.7 copy-start.44
  (48 other events, 260.4 us)
Sparse Core Ops, SparseCore 0:
  10.9 158.9 all-gather.6
  172.8 90.7 all-gather.8
  266.4 152.7 all-gather.10
  421.9 142.7 all-gather.12
  567.4 142.7 all-gather.14
  901.1 129.6 reduce-scatter.18
  1033.7 185.0 reduce-scatter.10
  1226.9 433.6 reduce-scatter.8
  1663.6 491.6 reduce-scatter.12
  2158.1 493.0 reduce-scatter.14
  2654.2 493.0 reduce-scatter.16
where the time goes:
time: 3160 us; the launch traced here: 3150 us
  waiting for transfers between devices  2590 us (82%)
  matrix products  238 us (8%)
  blocking collectives  147 us (5%)
  local copies, waits for them, and re-layouts  88.9 us (3%)
  starting transfers between devices  43.1 us (1%)
    reduce_scatter x2, waiting for transfers between devices, reduce_full(): lax.psum_scatter(first_w, ('seq', 'fsdp'), scatter_dimension=0, tiled=True)  936 us
    reduce_scatter x2, waiting for transfers between devices, reduce_full(): lax.psum_scatter(last_w, ('seq', 'fsdp'), scatter_dimension=0, tiled=True)  650 us
    reduce_scatter x1, waiting for transfers between devices, reduce_full(): lax.psum_scatter(middle_w, ('seq', 'fsdp'), scatter_dimension=0, tiled=True)  496 us
    all_gather x2, waiting for transfers between devices, fetch_full(): lax.all_gather(first_w, ('seq', 'fsdp'), axis=0, tiled=True)  151 us
    all_gather x2, waiting for transfers between devices, fetch_full(): lax.all_gather(last_w, ('seq', 'fsdp'), axis=0, tiled=True)  133 us
    all_gather x1, waiting for transfers between devices, fetch_full(): lax.all_gather(middle_w, ('seq', 'fsdp'), axis=0, tiled=True)  133 us
    dot_general x5, matrix products, outer(): lax.dot_general(left, right, (((0,), (0,)), ((), ())), preferred_element_...  82.9 us
    unnamed x2, blocking collectives  82.4 us
  transfers between devices with their start and end apart: 18, of which 16 were waited for; matrix products, arithmetic and copies ran while one was open for 7% of the time, Pallas kernels for 0%

commit v1 on v0

--- a/solution.py
+++ b/solution.py
@@ -6,6 +6,20 @@
 HEAD_DIM = 64
 ROT = 16
 EPS = 1e-05
+
+
+def see_the_cube(x_part, mesh_name, join_dim):
+    local_part, block_now = (lax.axis_size(mesh_name), lax.axis_index(mesh_name))
+    reply, state_now = (x_part, 1)
+    while state_now < local_part:
+        far_arr = lax.ppermute(
+            reply, mesh_name, tuple(((w, w ^ state_now) for w in range(local_part)))
+        )
+        local_next = jnp.concatenate([reply, far_arr], join_dim)
+        item_now = jnp.concatenate([far_arr, reply], join_dim)
+        reply = jnp.where(block_now & state_now == 0, local_next, item_now)
+        state_now = 2 * state_now
+    return reply
 
 
 def normalize(values):
@@ -150,7 +164,7 @@
             lax.all_gather(gain, ("seq", "fsdp"), axis=0, tiled=True),
             lax.all_gather(shift, ("seq", "fsdp"), axis=0, tiled=True),
             lax.all_gather(first_w, ("seq", "fsdp"), axis=0, tiled=True),
-            lax.all_gather(middle_w, ("seq", "fsdp"), axis=0, tiled=True),
+            see_the_cube(middle_w, ("seq", "fsdp"), 0),
             lax.all_gather(last_w, ("seq", "fsdp"), axis=0, tiled=True),
         )
 

time: 3160 us -> 3640 us (1.15)
  waiting for transfers between devices: 2590 us -> 3040 us
    all_to_all x1, waiting for transfers between devices: 27.9 us -> 545 us  [body(): lax.all_to_all(mixed_pack[order].astype(jnp.bfloat16), 'seq', split_axis=...]
    ppermute x0 -> x10, waiting for transfers between devices: none -> 359 us  [see_the_cube(): lax.ppermute(reply, mesh_name, tuple(((w, w ^ state_now) for w in range(l...]
    all_gather x2, waiting for transfers between devices: 151 us -> 0.04 us  [fetch_full(): lax.all_gather(first_w, ('seq', 'fsdp'), axis=0, tiled=True)]
    all_gather x2, waiting for transfers between devices: 133 us -> 0.02 us  [fetch_full(): lax.all_gather(last_w, ('seq', 'fsdp'), axis=0, tiled=True)]
    all_gather x1 -> x0, waiting for transfers between devices: 133 us -> none  [fetch_full(): lax.all_gather(middle_w, ('seq', 'fsdp'), axis=0, tiled=True)]
    all_gather x1 -> x0, blocking collectives: 43.8 us -> none  [fetch_full(): lax.all_gather(middle_w, ('seq', 'fsdp'), axis=0, tiled=True)]
  transfers between devices with their start and end apart: 18 -> 27, of which waited for: 16 -> 16; matrix products, arithmetic and copies ran while one was open for 7% -> 7% of each run, Pallas kernels for 0% -> 0%
where the time goes in v1:
time: 3640 us; the launch traced here: 3630 us
  waiting for transfers between devices  3040 us (84%)
  matrix products  252 us (7%)
  blocking collectives  114 us (3%)
  local copies, waits for them, and re-layouts  89.3 us (2%)
  starting transfers between devices  57.9 us (2%)
  other arithmetic  52.8 us (1%)
    reduce_scatter x2, waiting for transfers between devices, reduce_full(): lax.psum_scatter(first_w, ('seq', 'fsdp'), scatter_dimension=0, tiled=True)  937 us
    reduce_scatter x2, waiting for transfers between devices, reduce_full(): lax.psum_scatter(last_w, ('seq', 'fsdp'), scatter_dimension=0, tiled=True)  650 us
    all_to_all x1, waiting for transfers between devices, body(): lax.all_to_all(mixed_pack[order].astype(jnp.bfloat16), 'seq', split_axis=...  545 us
    reduce_scatter x1, waiting for transfers between devices, reduce_full(): lax.psum_scatter(middle_w, ('seq', 'fsdp'), scatter_dimension=0, tiled=True)  496 us
    ppermute x10, waiting for transfers between devices, see_the_cube(): lax.ppermute(reply, mesh_name, tuple(((w, w ^ state_now) for w in range(l...  359 us
    unnamed x2, blocking collectives  92.9 us
    dot_general x5, matrix products, outer(): lax.dot_general(left, right, (((0,), (0,)), ((), ())), preferred_element_...  83 us
  transfers between devices with their start and end apart: 27, of which 16 were waited for; matrix products, arithmetic and copies ran while one was open for 7% of the time, Pallas kernels for 0%

profile of v1, /device:TPU:1, one launch (start us, length us, event | category | flops | bytes accessed | tf_op | source)
XLA Modules:
  0.0 3628.4 jit_solution(10556095188077278237)
XLA Ops:
  16.5 38.0 %collective-permute-done.6 = bf16[128,5632]{1,0:T(8,128)(2,1)S(1)} collective-permute-done((bf16[128,5632]{1,0:T(8,128)(2,1)S(1)}, bf16[128,5632]{1,0:T(8,128)(2,1)S(1)}, u32[]{:S(2)}, u32[]{:S(2)}) %collective-permute-start.6) | collective-permute-done | bytes 1441824 | tf_op jit(solution)/shard_map/ppermute | solution.py:15
  66.4 83.9 %collective-permute-done.7 = bf16[256,5632]{1,0:T(8,128)(2,1)} collective-permute-done((bf16[256,5632]{1,0:T(8,128)(2,1)}, bf16[256,5632]{1,0:T(8,128)(2,1)}, u32[]{:S(2)}, u32[]{:S(2)}) %collective-permute-start.7) | collective-permute-done | bytes 2883616 | tf_op jit(solution)/shard_map/ppermute | solution.py:15
  160.3 233.4 %collective-permute-done.3 = bf16[512,3]{0,1:T(4,128)(2,1)S(1)} collective-permute-done((bf16[512,3]{0,1:T(4,128)(2,1)S(1)}, bf16[512,3]{0,1:T(4,128)(2,1)S(1)}, u32[]{:S(2)}, u32[]{:S(2)}) %collective-permute-start.3) | collective-permute-done | bytes 3104 | tf_op jit(solution)/shard_map/ppermute | solution.py:15
  400.9 48.6 %all-reduce.9 = (bf16[2048]{0:T(1024)(128)(2,1)S(1)}, bf16[2048]{0:T(1024)(128)(2,1)S(1)}, bf16[2048]{0:T(1024)(128)(2,1)S(1)}, bf16[2048]{0:T(1024)(128)(2,1)S(1)}) all-reduce(bf16[2048]{0:T(1024)(128)(2,1)S(1)} %dynamic-update-slice.1, bf16[2048]{0:T(1024)(128)(2,1)S(1)} %dynamic-update-slice, ...), channel_id=1, replica_groups=mesh['seq'=8,'fsdp'=4] {'seq','fsdp'}, use_global_device_ids=true, to_apply=%add.1 | all-reduce | flops 8192 | bytes 32768
  450.1 10.4 convolution_add_fusion
  467.2 20.9 all_to_all.116
  488.1 11.3 all-to-all-start.1
  506.1 12.6 all-to-all-done.1
  522.5 16.4 maximum_select_fusion.1
  554.2 22.6 while.30
  592.2 13.9 fusion.61
  606.1 544.9 %all-to-all-done.3 = bf16[8,128,256]{1,2,0:T(8,128)(2,1)S(1)} async-done(((bf16[8,128,256]{1,2,0:T(8,128)(2,1)}), bf16[8,128,256]{1,2,0:T(8,128)(2,1)S(1)}, u32[]{:S(2)}, u32[]{:S(2)}) %all-to-all-start.3) | async-done | bytes 524320 | tf_op jit(solution)/shard_map/all_to_all | solution.py:208
  1158.2 12.5 fusion.81
  1170.7 19.2 multiply_convert_fusion.1
  1189.9 13.9 fusion.82
  1203.8 17.8 fusion.38
  1221.7 12.8 fusion.56
  1247.6 13.4 all-to-all-done.4
  1268.9 44.1 %while.31 = (s32[]{:T(128)}, bf16[1024,4,64]{0,2,1:T(8,128)(2,1)}, f32[1024,4,64]{0,2,1:T(8,128)S(1)}, f32[1024,4,64]{0,2,1:T(8,128)}, s32[1024]{0:T(1024)S(1)},...) while((s32[]{:T(128)}, bf16[1024,4,64]{0,2,1:T(8,128)(2,1)}, ...), condition=%wide.region_18.19_spmd.clone, body=%wide.region_16.18_spmd.clone.sunk | while | flops 1378222080 | bytes 164707824 | solution.py:288
  1328.2 8.3 all-to-all-done.6
  1360.4 12.8 all-to-all-done.7
  1384.4 20.8 fusion.74
  1406.7 18.0 fusion.83
  1426.1 18.0 fusion.84
  1445.6 18.1 fusion.59
  1465.0 20.6 fusion.54
  1485.6 44.3 %all-reduce.8 = (f32[2048]{0:T(1024)S(1)}, f32[2048]{0:T(1024)S(1)}, f32[2048]{0:T(1024)S(1)}, f32[2048]{0:T(1024)S(1)}, f32[1]{0:T(128)}, /*index=5*/f32[1]{0:T(128)}, f32[1]{0:T(128)}) all-reduce(f32[2048]{0:T(1024)S(1)} %get-tuple-element.310, ...), channel_id=2, replica_groups=mesh['seq'=8,'fsdp'=4] {'seq','fsdp'}, use_global_device_ids=true, to_apply=%region_22.23.clone | all-reduce | flops 8195 | bytes 65560
  1538.8 153.8 %reduce-scatter.11.cloned.1.call-done = f32[64,2048]{1,0:T(8,128)} async-done(((f32[2048,2048]{1,0:T(8,128)}), f32[64,2048]{1,0:T(8,128)}) %reduce-scatter.11.cloned.1.call-update) | async-done | bytes 524304 | tf_op jit(solution)/shard_map/reduce_scatter | solution.py:177
  1692.6 441.9 %reduce-scatter.9.cloned.1.call-done = f32[64,6144]{1,0:T(8,128)} async-done(((f32[2048,6144]{1,0:T(8,128)}), f32[64,6144]{1,0:T(8,128)}) %reduce-scatter.9.cloned.1.call-update) | async-done | bytes 1572880 | tf_op jit(solution)/shard_map/reduce_scatter | solution.py:175
  2134.5 494.7 %reduce-scatter.13.cloned.1.call-done = f32[64,5632]{1,0:T(8,128)} async-done(((f32[2048,5632]{1,0:T(8,128)}), f32[64,5632]{1,0:T(8,128)}) %reduce-scatter.13.cloned.1.call-update) | async-done | bytes 1441808 | tf_op jit(solution)/shard_map/reduce_scatter | solution.py:175
  2629.2 496.1 %reduce-scatter.15.cloned.1.call-done = f32[64,5632]{1,0:T(8,128)} async-done(((f32[2048,5632]{1,0:T(8,128)}), f32[64,5632]{1,0:T(8,128)}) %reduce-scatter.15.cloned.1.call-update) | async-done | bytes 1441808 | tf_op jit(solution)/shard_map/reduce_scatter | solution.py:176
  3125.3 495.9 %reduce-scatter.17.cloned.1.call-done = f32[176,2048]{1,0:T(8,128)} async-done(((f32[5632,2048]{1,0:T(8,128)}), f32[176,2048]{1,0:T(8,128)}) %reduce-scatter.17.cloned.1.call-update) | async-done | bytes 1441808 | tf_op jit(solution)/shard_map/reduce_scatter | solution.py:177
  (340 shorter events, 241.7 us)
Async XLA Ops:
  7.2 442.4 %all-gather.5.cloned.1.call-start = ((), (), s32[]{:S(2)}) async-start(), calls=%async_computation.14 | async-start | bytes 25952256 | tf_op jit(solution)/shard_map/all_gather | solution.py:166
  8.0 584.3 %all-gather.11.cloned.1.call-start = ((), (), s32[]{:S(2)}) async-start(), calls=%async_computation.17 | async-start | bytes 23789568 | tf_op jit(solution)/shard_map/all_gather | solution.py:168
  8.7 597.4 %all-gather.7.cloned.1.call-start = ((), (), s32[]{:S(2)}) async-start(), calls=%async_computation.15 | async-start | bytes 8650752 | tf_op jit(solution)/shard_map/all_gather | solution.py:168
  9.4 1148.8 %all-gather.9.cloned.1.call-start = ((), (), s32[]{:S(2)}) async-start(), calls=%async_computation.16 | async-start | bytes 23789568 | tf_op jit(solution)/shard_map/all_gather | solution.py:166
  10.0 2.5 collective-permute-start.5
  14.1 40.4 %collective-permute-start.6 = (bf16[128,5632]{1,0:T(8,128)(2,1)S(1)}, bf16[128,5632]{1,0:T(8,128)(2,1)S(1)}, u32[]{:S(2)}, u32[]{:S(2)}) collective-permute-start(bf16[128,5632]{1,0:T(8,128)(2,1)S(1)} %maximum_select_fusion.8), channel_id=1, source_target_pairs={{0,2},{1,3},{2,0},{3,1},{4,6},{5,7},{6,4},{7,5},{8,10},{9,11},{10,... | collective-permute-start | bytes 4325384 | tf_op jit(solution)/shard_map/ppermute | solution.py:15
  56.5 93.9 %collective-permute-start.7 = (bf16[256,5632]{1,0:T(8,128)(2,1)}, bf16[256,5632]{1,0:T(8,128)(2,1)}, u32[]{:S(2)}, u32[]{:S(2)}) collective-permute-start(bf16[256,5632]{1,0:T(8,128)(2,1)} %maximum_select_fusion.5), channel_id=1, source_target_pairs={{0,4},{1,5},{2,6},{3,7},{4,0},{5,1},{6,2},{7,3},{8,12},{9,13},{10,... | collective-permute-start | bytes 8650760 | tf_op jit(solution)/shard_map/ppermute | solution.py:15
  57.6 4.7 collective-permute-start
  62.3 402.9 %copy-start.42 = (f32[128,8]{0,1:T(8,128)}, f32[128,8]{0,1:T(8,128)S(1)}, u32[]{:S(2)}) copy-start(f32[128,8]{0,1:T(8,128)S(1)} %get-tuple-element.405) | copy-start | bytes 12292
  62.4 3.5 collective-permute-start.1
  65.9 334.0 %copy-start.55 = (bf16[64]{0:T(256)(128)(2,1)S(1)}, bf16[64]{0:T(256)(128)(2,1)}, u32[]{:S(2)}) copy-start(bf16[64]{0:T(256)(128)(2,1)} %param.20) | copy-start | bytes 388
  65.9 334.2 %copy-start.56 = (bf16[64]{0:T(256)(128)(2,1)S(1)}, bf16[64]{0:T(256)(128)(2,1)}, u32[]{:S(2)}) copy-start(bf16[64]{0:T(256)(128)(2,1)} %param.19) | copy-start | bytes 388
  65.9 334.5 %copy-start.57 = (bf16[64]{0:T(256)(128)(2,1)S(1)}, bf16[64]{0:T(256)(128)(2,1)}, u32[]{:S(2)}) copy-start(bf16[64]{0:T(256)(128)(2,1)} %param.25) | copy-start | bytes 388
  65.9 334.7 %copy-start.58 = (bf16[64]{0:T(256)(128)(2,1)S(1)}, bf16[64]{0:T(256)(128)(2,1)}, u32[]{:S(2)}) copy-start(bf16[64]{0:T(256)(128)(2,1)} %param.24) | copy-start | bytes 388
  65.9 93.8 %collective-permute-start.2 = (bf16[256,3]{0,1:T(4,128)(2,1)S(1)}, bf16[256,3]{0,1:T(4,128)(2,1)S(1)}, u32[]{:S(2)}, u32[]{:S(2)}) collective-permute-start(bf16[256,3]{0,1:T(4,128)(2,1)S(1)} %maximum_select_fusion.12), channel_id=1, source_target_pairs={{0,4},{1,5},{2,6},{3,7},{4,0},{5,1},{6,2},{7,3},{8,12},{9,13},{10,... | collective-permute-start | bytes 4616 | tf_op jit(solution)/shard_map/ppermute | solution.py:15
  158.5 364.0 %collective-permute-start.8 = (bf16[512,5632]{1,0:T(8,128)(2,1)}, bf16[512,5632]{1,0:T(8,128)(2,1)}, u32[]{:S(2)}, u32[]{:S(2)}) collective-permute-start(bf16[512,5632]{1,0:T(8,128)(2,1)} %maximum_select_fusion.2), channel_id=1, source_target_pairs={{0,8},{1,9},{2,10},{3,11},{4,12},{5,13},{6,14},{7,15},{8,0},{9,1},... | collective-permute-start | bytes 17301512 | tf_op jit(solution)/shard_map/ppermute | solution.py:15
  159.7 233.9 %collective-permute-start.3 = (bf16[512,3]{0,1:T(4,128)(2,1)S(1)}, bf16[512,3]{0,1:T(4,128)(2,1)S(1)}, u32[]{:S(2)}, u32[]{:S(2)}) collective-permute-start(bf16[512,3]{0,1:T(4,128)(2,1)S(1)} %maximum_select_fusion.11), channel_id=1, source_target_pairs={{0,8},{1,9},{2,10},{3,11},{4,12},{5,13},{6,14},{7,15},{8,0},{9,1},... | collective-permute-start | bytes 9224 | tf_op jit(solution)/shard_map/ppermute | solution.py:15
  393.7 55.9 %collective-permute-start.4 = (bf16[1024,3]{0,1:T(4,128)(2,1)S(1)}, bf16[1024,3]{0,1:T(4,128)(2,1)S(1)}, u32[]{:S(2)}, u32[]{:S(2)}) collective-permute-start(bf16[1024,3]{0,1:T(4,128)(2,1)S(1)} %maximum_select_fusion.10), channel_id=1, source_target_pairs={{0,16},{1,17},{2,18},{3,19},{4,20},{5,21},{6,22},{7,23},{8,24},{9,... | collective-permute-start | bytes 18440 | tf_op jit(solution)/shard_map/ppermute | solution.py:15
  488.1 30.6 all-to-all-start.1
  518.7 31.4 all-to-all-start.2
  538.9 631.8 %collective-permute-start.9 = (bf16[1024,5632]{1,0:T(8,128)(2,1)}, bf16[1024,5632]{1,0:T(8,128)(2,1)}, u32[]{:S(2)}, u32[]{:S(2)}) collective-permute-start(bf16[1024,5632]{1,0:T(8,128)(2,1)} %maximum_select_fusion.1), channel_id=1, source_target_pairs={{0,16},{1,17},{2,18},{3,19},{4,20},{5,21},{6,22},{7,23},{8,24},{9,... | collective-permute-start | bytes 34603016 | tf_op jit(solution)/shard_map/ppermute | solution.py:15
  588.3 562.7 %all-to-all-start.3 = ((bf16[8,128,256]{1,2,0:T(8,128)(2,1)}), bf16[8,128,256]{1,2,0:T(8,128)(2,1)S(1)}, u32[]{:S(2)}, u32[]{:S(2)}) async-start(bf16[8,128,256]{1,2,0:T(8,128)(2,1)} %copy.92), calls=%async_computation.3 | async-start | bytes 1048576 | tf_op jit(solution)/shard_map/all_to_all | solution.py:208
  1243.2 17.8 all-to-all-start.4
  1318.1 18.4 all-to-all-start.6
  1336.5 18.4 all-to-all-start.5
  1355.0 18.3 all-to-all-start.7
  1359.8 177.6 %reduce-scatter.19.cloned.1.call-start = ((), (), s32[]{:S(2)}) async-start(), calls=%async_computation.23 | async-start | bytes 1081344
  1375.2 317.4 %reduce-scatter.11.cloned.1.call-start = ((), (), s32[]{:S(2)}) async-start(), calls=%async_computation.19 | async-start | bytes 17301504 | tf_op jit(solution)/shard_map/reduce_scatter | solution.py:177
  1383.4 751.1 %reduce-scatter.9.cloned.1.call-start = ((), (), s32[]{:S(2)}) async-start(), calls=%async_computation.18 | async-start | bytes 51904512 | tf_op jit(solution)/shard_map/reduce_scatter | solution.py:175
  1405.3 1223.9 %reduce-scatter.13.cloned.1.call-start = ((), (), s32[]{:S(2)}) async-start(), calls=%async_computation.20 | async-start | bytes 47579136 | tf_op jit(solution)/shard_map/reduce_scatter | solution.py:175
  1424.8 1700.5 %reduce-scatter.15.cloned.1.call-start = ((), (), s32[]{:S(2)}) async-start(), calls=%async_computation.21 | async-start | bytes 47579136 | tf_op jit(solution)/shard_map/reduce_scatter | solution.py:176
  1444.1 2177.0 %reduce-scatter.17.cloned.1.call-start = ((), (), s32[]{:S(2)}) async-start(), calls=%async_computation.22 | async-start | bytes 47579136 | tf_op jit(solution)/shard_map/reduce_scatter | solution.py:177
  (63 other events, 1120.1 us)
Sparse Core Ops, SparseCore 0:
  10.9 206.1 all-gather.4
  220.0 204.8 all-gather.10
  427.7 91.4 all-gather.6
  521.9 446.6 all-gather.8
  1375.3 129.4 reduce-scatter.18
  1507.6 184.9 reduce-scatter.10
  1700.8 433.6 reduce-scatter.8
  2137.5 491.6 reduce-scatter.12
  2632.2 493.0 reduce-scatter.14
  3128.1 493.0 reduce-scatter.16
